TPU v7x, 512 devices: a whole 4x8x8 slice. The times are simulated.
512 devices in a mesh: tok: 16 (over z, core), voc: 32 (over y, x).
Axes of the slice: x: 4, y: 8, z: 8, core: 2. Of those that a mesh axis runs over, the one named last changes fastest.
Arguments:
- hidden: bfloat16 [256, 2304], P('tok', 'voc'), may hold values from -18 to 18
- head: bfloat16 [2304, 131072], P(None, ('tok', 'voc')), as said below
- targets: int32 [256], replicated, may hold values from 0 to 131071
- probe_hidden: bfloat16 [256, 2304], P('tok', 'voc'), may hold values from -6 to 6
- probe_head: bfloat16 [2304, 131072], P(None, ('tok', 'voc')), may hold values from -0.5 to 0.5
Outputs:
- head_out: float32 [2304, 131072], P(None, ('tok', 'voc'))
- hidden_out: float32 [256, 2304], P('tok', 'voc')
Inputs may be any that keep to these rules, and one draw needn't show every extreme that they name: `head`: entries lie within 66 / sqrt(2304) in magnitude.
All inputs are finite; a program needn't handle non-finite values.
Results may differ from a plain program's by a relative error of at most 0.0075.
Values may be sent and summed in bfloat16 or wider, within the bound.
A program may use at most 64 MiB of HBM per device.

v0:
```python
import jax
import jax.numpy as jnp
from jax import lax
from jax.sharding import PartitionSpec as P

softcap_value = 30.0
zloss_weight = 0.0001


def local(hidden, head, targets, probe_hidden, probe_head):
    voc_count = lax.axis_size("voc")
    vocab_width = head.shape[1]
    stacked = jnp.stack([hidden, probe_hidden])
    features = lax.all_gather(stacked, "voc", axis=2, tiled=True)
    gathered = lax.all_gather(features, "tok", axis=1, tiled=True)
    row_hidden = gathered[0]
    row_probe = gathered[1]
    logits = jnp.dot(row_hidden, head, preferred_element_type=jnp.float32)
    tangent = jnp.dot(row_probe, head, preferred_element_type=jnp.float32) + jnp.dot(
        row_hidden, probe_head, preferred_element_type=jnp.float32
    )
    capped = jnp.tanh(logits / softcap_value)
    cap_slope = 1.0 - capped * capped
    exponent = jnp.exp(softcap_value * capped)
    cap_tangent = cap_slope * tangent
    stats = lax.psum(
        jnp.stack([jnp.sum(exponent, axis=1), jnp.sum(exponent * cap_tangent, axis=1)]),
        ("tok", "voc"),
    )
    row_total = stats[0]
    probability = exponent / row_total[:, None]
    mean_tangent = stats[1] / row_total
    factor = 1.0 + 2.0 * zloss_weight * jnp.log(row_total)
    offset = (lax.axis_index("tok") * voc_count + lax.axis_index("voc")) * vocab_width
    columns = offset + lax.iota(jnp.int32, vocab_width)
    onehot = (targets[:, None] == columns[None, :]).astype(jnp.float32)
    grad_cap = factor[:, None] * probability - onehot
    grad_tan = probability * (
        factor[:, None] * (cap_tangent - mean_tangent[:, None])
        + 2.0 * zloss_weight * mean_tangent[:, None]
    )
    slope_tan = -2.0 / softcap_value * capped * cap_slope * tangent
    dlogit = (grad_cap * cap_slope).astype(jnp.bfloat16)
    dlogit_tan = (grad_tan * cap_slope + grad_cap * slope_tan).astype(jnp.bfloat16)
    head_out = jnp.einsum(
        "krd,krv->dv", gathered, jnp.stack([dlogit_tan, dlogit]), preferred_element_type=jnp.float32
    )
    probe_part = lax.dot_general(
        dlogit, probe_head, (((1,), (1,)), ((), ())), preferred_element_type=jnp.float32
    )
    head_part = lax.dot_general(
        dlogit_tan, head, (((1,), (1,)), ((), ())), preferred_element_type=jnp.float32
    )
    summed = lax.psum_scatter(probe_part + head_part, "tok", scatter_dimension=0, tiled=True)
    hidden_out = lax.psum_scatter(summed, "voc", scatter_dimension=1, tiled=True)
    return (head_out, hidden_out)


def solution(mesh):
    return jax.shard_map(
        local,
        mesh=mesh,
        in_specs=(
            P("tok", "voc"),
            P(None, ("tok", "voc")),
            P(),
            P("tok", "voc"),
            P(None, ("tok", "voc")),
        ),
        out_specs=(P(None, ("tok", "voc")), P("tok", "voc")),
        check_vma=False,
    )
```

profile of v0, /device:TPU:2, one launch (start us, length us, event | category | flops | bytes accessed | tf_op | source)
XLA Modules:
  0.0 435.7 jit_solution(9446589212632024018)
XLA Ops:
  7.2 0.0 copy-start
  7.2 0.0 all-gather.2.cloned.1.call-start
  7.2 0.8 pad_maximum_fusion
  8.0 0.1 copy.12
  8.1 52.7 %all_gather.6 = bf16[2,16,2304]{1,0,2:T(2,128)(2,1)S(1)} all-gather(bf16[2,16,72]{1,0,2:T(2,128)(2,1)S(1)} %copy.12), channel_id=1, replica_groups=mesh['tok'=16,'voc'=32] {'voc'}, dimensions={2}, use_global_device_ids=true | all-gather | bytes 152064 | tf_op jit(solution)/shard_map/all_gather | solution.py:14
  60.8 2.2 copy.13
  63.0 0.0 all-gather.2.cloned.1.call-update
  63.0 0.0 reduce-scatter.3.cloned.1.call-start
  63.1 43.3 %all-gather.2.cloned.1.call-done = bf16[2,256,2304]{2,1,0:T(8,128)(2,1)} async-done(((bf16[2,16,2304]{2,1,0:T(8,128)(2,1)}), bf16[2,256,2304]{2,1,0:T(8,128)(2,1)}) %all-gather.2.cloned.1.call-update) | async-done | bytes 2359312 | tf_op jit(solution)/shard_map/all_gather | solution.py:15
  106.4 0.0 copy-start.1
  106.4 2.4 fusion.3
  108.7 0.0 copy-done
  108.7 0.0 copy-done.1
  108.7 0.6 fusion.1
  109.3 0.0 copy-start.4
  109.4 0.0 copy-start.5
  109.4 1.3 fusion.9
  110.7 0.0 copy-done.4
  110.7 96.8 %psum.7 = f32[2,256]{1,0:T(2,128)S(1)} all-reduce(f32[2,256]{1,0:T(2,128)S(1)} %pad_maximum_fusion.1), channel_id=1, replica_groups=mesh['tok'=16,'voc'=32] {'tok','voc'}, use_global_device_ids=true, to_apply=%region_2.0 | all-reduce | flops 512 | bytes 4096 | tf_op jit(solution)/shard_map/psum | solution.py:26
  207.5 0.0 copy-done.5
  207.5 1.2 add_convert_fusion
  208.7 0.0 copy-start.3
  208.8 0.0 copy-start.2
  208.8 1.9 fusion.12
  210.7 0.0 copy-done.3
  210.7 0.0 copy-done.2
  210.7 2.0 convolution_add_fusion
  212.6 0.0 reduce-scatter.3.cloned.1.call-update
  212.7 0.0 all-reduce.3.cloned.1.call-start
  212.7 1.3 dynamic-slice
  214.6 57.4 %reduce-scatter.3.cloned.1.call-done = f32[16,2304]{1,0:T(8,128)} async-done(((f32[256,2304]{1,0:T(8,128)}), f32[16,2304]{1,0:T(8,128)}) %reduce-scatter.3.cloned.1.call-update) | async-done | bytes 147472 | tf_op jit(solution)/shard_map/reduce_scatter | solution.py:54
  272.0 0.0 all-reduce.3.cloned.1.call-update
  272.1 3.2 convolution_bitcast_fusion
  275.3 152.5 %all-reduce.3.cloned.1.call-done = f32[16,2304]{1,0:T(8,128)} async-done(((f32[16,2304]{1,0:T(8,128)}), f32[16,2304]{1,0:T(8,128)}) %all-reduce.3.cloned.1.call-update) | async-done | bytes 147472
  427.8 1.4 constant_dynamic-slice_fusion
  (4 shorter events, 0.0 us)
Async XLA Ops:
  7.2 101.6 %copy-start = (bf16[2304,256]{1,0:T(8,128)(2,1)S(1)}, bf16[2304,256]{1,0:T(8,128)(2,1)}, u32[]{:S(2)}) copy-start(bf16[2304,256]{1,0:T(8,128)(2,1)} %param.6) | copy-start | bytes 3538948
  7.2 99.2 %all-gather.2.cloned.1.call-start = ((), (), s32[]{:S(2)}) async-start(), calls=%async_computation.1 | async-start | bytes 2506752 | tf_op jit(solution)/shard_map/all_gather | solution.py:15
  63.0 209.0 %reduce-scatter.3.cloned.1.call-start = ((), (), s32[]{:S(2)}) async-start(), calls=%async_computation.2 | async-start | bytes 2506752 | tf_op jit(solution)/shard_map/reduce_scatter | solution.py:54
  106.4 2.4 copy-start.1
  109.3 1.3 copy-start.4
  109.4 98.1 %copy-start.5 = (s32[256]{0:T(256)S(1)}, s32[256]{0:T(256)}, u32[]{:S(2)}) copy-start(s32[256]{0:T(256)} %param.7) | copy-start | bytes 3076
  208.7 1.9 copy-start.3
  208.8 1.9 copy-start.2
  212.7 215.1 %all-reduce.3.cloned.1.call-start = ((), (), s32[]{:S(2)}) async-start(), calls=%async_computation.3 | async-start | bytes 294912
Sparse Core Ops, SparseCore 0:
  63.1 43.1 all-gather.1
  212.8 59.2 reduce-scatter.2
  275.5 152.2 all-reduce.2
where the time goes:
time: 436 us
  waiting for transfers between devices  253 us (58%)
  blocking collectives  149 us (34%)
  between operations  14.5 us (3%)
  matrix products  11.3 us (3%)
  local copies, waits for them, and re-layouts  5.01 us (1%)
    unnamed x4, waiting for transfers between devices  153 us
    psum x1, blocking collectives, local(): lax.psum(jnp.stack([jnp.sum(exponent, axis=1), jnp.sum(exponent * cap_tan...  96.8 us
    reduce_scatter x1, waiting for transfers between devices, local(): lax.psum_scatter(probe_part + head_part, 'tok', scatter_dimension=0, tile...  57.4 us
    all_gather x1, blocking collectives, local(): features = lax.all_gather(stacked, 'voc', axis=2, tiled=True)  52.7 us
    all_gather x1, waiting for transfers between devices, local(): gathered = lax.all_gather(features, 'tok', axis=1, tiled=True)  43.3 us
  transfers between devices with their start and end apart: 3, of which 3 were waited for; matrix products, arithmetic and copies ran while one was open for 1% of the time, Pallas kernels for 0%

commit v1 on v0

--- a/solution.py
+++ b/solution.py
@@ -11,7 +11,9 @@
     voc_count = lax.axis_size("voc")
     vocab_width = head.shape[1]
     stacked = jnp.stack([hidden, probe_hidden])
-    features = lax.all_gather(stacked, "voc", axis=2, tiled=True)
+    features = jnp.concatenate(
+        lax.all_to_all(jnp.stack([stacked] * lax.axis_size("voc")), "voc", 0, 0), axis=2
+    )
     gathered = lax.all_gather(features, "tok", axis=1, tiled=True)
     row_hidden = gathered[0]
     row_probe = gathered[1]

time: 436 us -> 403 us (0.924)
  blocking collectives: 149 us -> 118 us
    all_gather x1 -> x0, blocking collectives: 52.7 us -> none  [local(): features = lax.all_gather(stacked, 'voc', axis=2, tiled=True)]
    all_to_all x0 -> x1, blocking collectives: none -> 21.3 us  [local(): lax.all_to_all(jnp.stack([stacked] * lax.axis_size('voc')), 'voc', 0, 0)]
where the time goes in v1:
time: 403 us
  waiting for transfers between devices  253 us (63%)
  blocking collectives  118 us (29%)
  between operations  14.5 us (4%)
  matrix products  11.3 us (3%)
    unnamed x4, waiting for transfers between devices  153 us
    psum x1, blocking collectives, local(): lax.psum(jnp.stack([jnp.sum(exponent, axis=1), jnp.sum(exponent * cap_tan...  96.8 us
    reduce_scatter x1, waiting for transfers between devices, local(): lax.psum_scatter(probe_part + head_part, 'tok', scatter_dimension=0, tile...  57.4 us
    all_gather x1, waiting for transfers between devices, local(): gathered = lax.all_gather(features, 'tok', axis=1, tiled=True)  43.2 us
    all_to_all x1, blocking collectives, local(): lax.all_to_all(jnp.stack([stacked] * lax.axis_size('voc')), 'voc', 0, 0)  21.3 us
  transfers between devices with their start and end apart: 3, of which 3 were waited for; matrix products, arithmetic and copies ran while one was open for 1% of the time, Pallas kernels for 0%

profile of v1, /device:TPU:2, one launch (start us, length us, event | category | flops | bytes accessed | tf_op | source)
XLA Modules:
  0.0 403.1 jit_solution(1497613488664171501)
XLA Ops:
  7.2 0.0 copy-start
  7.2 0.0 all-gather.2.cloned.1.call-start
  7.2 0.8 pad_maximum_fusion
  8.1 21.3 %all_to_all.5 = bf16[32,2,16,72]{3,2,1,0:T(8,128)(2,1)S(1)} all-to-all(bf16[32,2,16,72]{3,2,1,0:T(8,128)(2,1)S(1)} %stack.23), channel_id=1, replica_groups=mesh['tok'=16,'voc'=32] {'voc'}, dimensions={0} | all-to-all | bytes 294912 | tf_op jit(solution)/shard_map/all_to_all | solution.py:15
  29.3 0.1 copy.8
  29.4 1.0 reshape.43
  30.4 0.0 all-gather.2.cloned.1.call-update
  30.5 0.0 reduce-scatter.3.cloned.1.call-start
  30.5 43.2 %all-gather.2.cloned.1.call-done = bf16[2,256,2304]{2,1,0:T(8,128)(2,1)} async-done(((bf16[2,16,2304]{2,1,0:T(8,128)(2,1)}), bf16[2,256,2304]{2,1,0:T(8,128)(2,1)}) %all-gather.2.cloned.1.call-update) | async-done | bytes 2359312 | tf_op jit(solution)/shard_map/all_gather | solution.py:17
  73.7 0.0 copy-start.1
  73.7 2.4 fusion.3
  76.1 0.0 copy-done
  76.1 0.0 copy-done.1
  76.1 0.6 fusion.1
  76.7 0.0 copy-start.4
  76.8 0.0 copy-start.5
  76.8 1.3 fusion.9
  78.1 0.0 copy-done.4
  78.1 96.8 %psum.7 = f32[2,256]{1,0:T(2,128)S(1)} all-reduce(f32[2,256]{1,0:T(2,128)S(1)} %pad_maximum_fusion.1), channel_id=1, replica_groups=mesh['tok'=16,'voc'=32] {'tok','voc'}, use_global_device_ids=true, to_apply=%region_2.0 | all-reduce | flops 512 | bytes 4096 | tf_op jit(solution)/shard_map/psum | solution.py:28
  174.9 0.0 copy-done.5
  174.9 1.2 add_convert_fusion
  176.1 0.0 copy-start.3
  176.1 0.0 copy-start.2
  176.2 1.9 fusion.12
  178.0 0.0 copy-done.3
  178.1 0.0 copy-done.2
  178.1 2.0 convolution_add_fusion
  180.0 0.0 reduce-scatter.3.cloned.1.call-update
  180.1 0.0 all-reduce.3.cloned.1.call-start
  180.1 1.3 dynamic-slice
  182.0 57.4 %reduce-scatter.3.cloned.1.call-done = f32[16,2304]{1,0:T(8,128)} async-done(((f32[256,2304]{1,0:T(8,128)}), f32[16,2304]{1,0:T(8,128)}) %reduce-scatter.3.cloned.1.call-update) | async-done | bytes 147472 | tf_op jit(solution)/shard_map/reduce_scatter | solution.py:56
  239.4 0.0 all-reduce.3.cloned.1.call-update
  239.4 3.2 convolution_bitcast_fusion
  242.7 152.5 %all-reduce.3.cloned.1.call-done = f32[16,2304]{1,0:T(8,128)} async-done(((f32[16,2304]{1,0:T(8,128)}), f32[16,2304]{1,0:T(8,128)}) %all-reduce.3.cloned.1.call-update) | async-done | bytes 147472
  395.1 1.4 constant_dynamic-slice_fusion
  (5 shorter events, 0.1 us)
Async XLA Ops:
  7.2 69.0 %copy-start = (bf16[2304,256]{1,0:T(8,128)(2,1)S(1)}, bf16[2304,256]{1,0:T(8,128)(2,1)}, u32[]{:S(2)}) copy-start(bf16[2304,256]{1,0:T(8,128)(2,1)} %param.6) | copy-start | bytes 3538948
  7.2 66.6 %all-gather.2.cloned.1.call-start = ((), (), s32[]{:S(2)}) async-start(), calls=%async_computation.2 | async-start | bytes 2506752 | tf_op jit(solution)/shard_map/all_gather | solution.py:17
  30.5 209.0 %reduce-scatter.3.cloned.1.call-start = ((), (), s32[]{:S(2)}) async-start(), calls=%async_computation.3 | async-start | bytes 2506752 | tf_op jit(solution)/shard_map/reduce_scatter | solution.py:56
  73.7 2.4 copy-start.1
  76.7 1.3 copy-start.4
  76.8 98.1 %copy-start.5 = (s32[256]{0:T(256)S(1)}, s32[256]{0:T(256)}, u32[]{:S(2)}) copy-start(s32[256]{0:T(256)} %param.7) | copy-start | bytes 3076
  176.1 1.9 copy-start.3
  176.1 1.9 copy-start.2
  180.1 215.1 %all-reduce.3.cloned.1.call-start = ((), (), s32[]{:S(2)}) async-start(), calls=%async_computation.4 | async-start | bytes 294912
Sparse Core Ops, SparseCore 0:
  30.6 43.1 all-gather.1
  180.2 59.2 reduce-scatter.2
  242.9 152.2 all-reduce.2
